TPU v7x, 32 devices: a whole 2x2x4 slice. The times are simulated.
32 devices in a mesh: grp: 2 (over x), inp: 4 (over y, core), out: 4 (over z).
Axes of the slice: x: 2, y: 2, z: 4, core: 2. Of those that a mesh axis runs over, the one named last changes fastest.
Arguments:
- activations: bfloat16 [4, 512, 8192], P('grp', 'out', 'inp'), parts along dimension 0, may hold values from -6 to 6
- out_grads: bfloat16 [4, 512, 28672], P('grp', 'inp', 'out'), parts along dimension 0, may hold values from -6 to 6
- query_grads: bfloat16 [2, 28672, 8192], P(None, 'out', 'inp'), may hold values from -0.00036621094 to 0.00036621094
- token_ids: int32 [4, 512], P('grp'), parts along dimension 0, may hold values from 0 to 128255
- loss_mask: int32 [4, 512], P('grp'), parts along dimension 0, may hold values 0 or 1
Outputs:
- scores: float32 [2, 4, 512], P(None, 'grp'), parts along dimension 1
There are 2 independent parts, one for each index of `grp`. A program takes and returns all parts, laid end to end along the dimension named above; an argument that names none is the same for every part. Nothing has to cross between parts.
All inputs are finite; a program needn't handle non-finite values.
Results may differ from a plain program's by a relative error of at most 0.0003.
Values may be sent and summed in bfloat16 or wider, within the bound.
A program may use at most 128 MiB of HBM per device.

v0:
```python
import jax
import jax.numpy as jnp
from jax import lax
from jax.sharding import PartitionSpec as P


def shards(activations, out_grads, query_grads, token_ids, loss_mask):
    blocks = activations.shape[0]
    partials = []
    for number in range(blocks):
        gathered = lax.all_gather(activations[number], "out", axis=0, tiled=True)
        projected = jnp.einsum(
            "to,qoi->tqi",
            lax.all_gather(out_grads[number], "inp", axis=0, tiled=True),
            query_grads,
            preferred_element_type=jnp.float32,
        )
        partial_value = jnp.sum(projected * gathered.astype(jnp.float32)[:, None, :], axis=2)
        partial_value = lax.psum(partial_value, ("inp", "out"))
        partials.append(partial_value)
    stacked = jnp.stack(partials)
    equal = token_ids[:, :, None] == token_ids[:, None, :]
    counts = jnp.sum(equal.astype(jnp.int32), axis=2)
    weight = loss_mask.astype(jnp.float32) / counts.astype(jnp.float32)
    return jnp.transpose(stacked * weight[:, :, None], (2, 0, 1))


def solution(mesh):
    in_specs = (
        P("grp", "out", "inp"),
        P("grp", "inp", "out"),
        P(None, "out", "inp"),
        P("grp", None),
        P("grp", None),
    )
    out_specs = P(None, "grp", None)
    return jax.shard_map(shards, mesh=mesh, in_specs=in_specs, out_specs=out_specs, check_vma=False)
```

profile of v0, /device:TPU:0, one launch (start us, length us, event | category | flops | bytes accessed | tf_op | source)
XLA Modules:
  0.0 289.7 jit_solution(5545557528172188764)
XLA Ops:
  6.5 0.0 copy-start
  6.5 0.0 copy-start.1
  6.5 0.0 all-gather.15.cloned.1.call-start
  6.5 2.3 fusion.10
  8.9 0.0 all-gather.15.cloned.1.call-update
  8.9 0.0 all-gather.11.cloned.1.call-start
  8.9 0.7 all-gather.11.cloned.1.call-update
  9.6 0.0 all-gather.13.cloned.1.call-start
  9.7 4.1 %fusion.9 = (bf16[1,128,7168]{2,1,0:T(8,128)(2,1)}, bf16[1,128,7168]{2,1,0:T(8,128)(2,1)}) fusion(bf16[2,128,7168]{2,1,0:T(8,128)(2,1)} %param.6), kind=kLoop, calls=%fused_computation.12 | loop fusion | bytes 7340032 | tf_op jit(solution)/shard_map/slice | solution.py:14
  13.8 0.0 all-gather.13.cloned.1.call-update
  13.8 0.0 all-gather.9.cloned.1.call-start
  13.9 0.5 all-gather.9.cloned.1.call-update
  14.4 0.0 copy-done
  14.4 0.4 convert_reduce_fusion
  14.8 0.0 copy-done.1
  14.8 42.6 %all-gather.15.cloned.1.call-done = bf16[1,512,2048]{2,1,0:T(8,128)(2,1)} async-done(((bf16[1,128,2048]{2,1,0:T(8,128)(2,1)}), bf16[1,512,2048]{2,1,0:T(8,128)(2,1)}) %all-gather.15.cloned.1.call-update) | async-done | bytes 2097168 | tf_op jit(solution)/shard_map/all_gather | solution.py:11
  57.4 4.1 %bitcast_convert_fusion = f32[512,2048]{1,0:T(8,128)} fusion(bf16[1,512,2048]{2,1,0:T(8,128)(2,1)} %all-gather.15.cloned.1.call-done), kind=kLoop, calls=%fused_computation.6 | loop fusion | flops 1048576 | bytes 6291456 | tf_op jit(solution)/shard_map/convert_element_type | solution.py:18
  61.5 42.0 %all-gather.11.cloned.1.call-done = bf16[1,512,2048]{2,1,0:T(8,128)(2,1)} async-done(((bf16[1,128,2048]{2,1,0:T(8,128)(2,1)}), bf16[1,512,2048]{2,1,0:T(8,128)(2,1)}) %all-gather.11.cloned.1.call-update) | async-done | bytes 2097168 | tf_op jit(solution)/shard_map/all_gather | solution.py:11
  103.5 4.1 %bitcast_convert_fusion.1 = f32[512,2048]{1,0:T(8,128)} fusion(bf16[1,512,2048]{2,1,0:T(8,128)(2,1)} %all-gather.11.cloned.1.call-done), kind=kLoop, calls=%fused_computation.7 | loop fusion | flops 1048576 | bytes 6291456 | tf_op jit(solution)/shard_map/convert_element_type | solution.py:18
  107.6 48.6 %all-gather.13.cloned.1.call-done = bf16[1,512,7168]{2,1,0:T(8,128)(2,1)} async-done(((bf16[1,128,7168]{2,1,0:T(8,128)(2,1)}), bf16[1,512,7168]{2,1,0:T(8,128)(2,1)}) %all-gather.13.cloned.1.call-update) | async-done | bytes 7340048 | tf_op jit(solution)/shard_map/all_gather | solution.py:14
  156.2 39.0 %multiply_reduce_fusion = f32[512,2]{0,1:T(2,128)S(1)} fusion(f32[512,2048]{1,0:T(8,128)} %bitcast_convert_fusion, bf16[2,7168,2048]{2,1,0:T(8,128)(2,1)} %param.7, bf16[1,512,7168]{2,1,0:T(8,128)(2,1)} %all-gather.13.cloned.1.call-done), kind=kOutput, calls=%fused_computation | convolution fusion | flops 30068965376 | bytes 70258688 | tf_op jit(solution)/shard_map/to,qoi->tqi/dot_general | solution.py:12
  195.2 14.8 %all-gather.9.cloned.1.call-done = bf16[1,512,7168]{2,1,0:T(8,128)(2,1)} async-done(((bf16[1,128,7168]{2,1,0:T(8,128)(2,1)}), bf16[1,512,7168]{2,1,0:T(8,128)(2,1)}) %all-gather.9.cloned.1.call-update) | async-done | bytes 7340048 | tf_op jit(solution)/shard_map/all_gather | solution.py:14
  210.0 38.8 %multiply_reduce_fusion.1 = f32[512,2]{0,1:T(2,128)S(1)} fusion(f32[512,2048]{1,0:T(8,128)} %bitcast_convert_fusion.1, bf16[2,7168,2048]{2,1,0:T(8,128)(2,1)} %param.7, bf16[1,512,7168]{2,1,0:T(8,128)(2,1)} %all-gather.9.cloned.1.call-done), kind=kOutput, calls=%fused_computation.1 | convolution fusion | flops 30068965376 | bytes 70258688 | tf_op jit(solution)/shard_map/to,qoi->tqi/dot_general | solution.py:12
  248.8 33.8 %all-reduce = (f32[1,512,2]{1,0,2:T(1,128)S(1)}, f32[1,512,2]{1,0,2:T(1,128)S(1)}) all-reduce(f32[1,512,2]{1,0,2:T(1,128)S(1)} %stack.10, f32[1,512,2]{1,0,2:T(1,128)S(1)} %stack.9), channel_id=1, replica_groups=mesh['grp'=2,'inp'=4,'out'=4] {'inp','out'}, use_global_device_ids=true, to_apply=%region_3.0 | all-reduce | flops 2048 | bytes 16384 | tf_op jit(solution)/shard_map/psum | solution.py:19
  282.6 0.6 fusion.8
  (3 shorter events, 0.0 us)
Async XLA Ops:
  6.5 7.9 %copy-start = (s32[2,512]{1,0:T(2,128)S(1)}, s32[2,512]{1,0:T(2,128)}, u32[]{:S(2)}) copy-start(s32[2,512]{1,0:T(2,128)} %param.8) | copy-start | bytes 12292
  6.5 8.3 %copy-start.1 = (s32[2,512]{1,0:T(2,128)S(1)}, s32[2,512]{1,0:T(2,128)}, u32[]{:S(2)}) copy-start(s32[2,512]{1,0:T(2,128)} %param.9) | copy-start | bytes 12292
  6.5 50.9 %all-gather.15.cloned.1.call-start = ((), (), s32[]{:S(2)}) async-start(), calls=%async_computation.3 | async-start | bytes 2621440 | tf_op jit(solution)/shard_map/all_gather | solution.py:11
  8.9 94.6 %all-gather.11.cloned.1.call-start = ((), (), s32[]{:S(2)}) async-start(), calls=%async_computation.1 | async-start | bytes 2621440 | tf_op jit(solution)/shard_map/all_gather | solution.py:11
  9.6 146.6 %all-gather.13.cloned.1.call-start = ((), (), s32[]{:S(2)}) async-start(), calls=%async_computation.2 | async-start | bytes 9175040 | tf_op jit(solution)/shard_map/all_gather | solution.py:14
  13.8 196.1 %all-gather.9.cloned.1.call-start = ((), (), s32[]{:S(2)}) async-start(), calls=%async_computation | async-start | bytes 9175040 | tf_op jit(solution)/shard_map/all_gather | solution.py:14
Sparse Core Ops, SparseCore 0:
  9.0 48.3 all-gather.14
  59.0 44.4 all-gather.10
  105.0 51.1 all-gather.12
  157.6 52.2 all-gather.8
where the time goes:
time: 290 us
  waiting for transfers between devices  149 us (51%)
  matrix products  77.8 us (27%)
  blocking collectives  33.8 us (12%)
  between operations  13.2 us (5%)
  other arithmetic  9.25 us (3%)
  local copies, waits for them, and re-layouts  6.45 us (2%)
    all_gather x2, waiting for transfers between devices, shards(): gathered = lax.all_gather(activations[number], 'out', axis=0, tiled=True)  84.5 us
    dot_general x2, matrix products, shards(): jnp.einsum('to,qoi->tqi', lax.all_gather(out_grads[number], 'inp', axis=0...  77.8 us
    all_gather x2, waiting for transfers between devices, shards(): lax.all_gather(out_grads[number], 'inp', axis=0, tiled=True)  63.4 us
    psum x1, blocking collectives, shards(): partial_value = lax.psum(partial_value, ('inp', 'out'))  33.8 us
    convert_element_type x2, other arithmetic, shards(): gathered.astype(jnp.float32)[:, None, :]  8.22 us
  transfers between devices with their start and end apart: 4, of which 4 were waited for; matrix products, arithmetic and copies ran while one was open for 18% of the time, Pallas kernels for 0%

commit v1 on v0

--- a/solution.py
+++ b/solution.py
@@ -2,6 +2,31 @@
 import jax.numpy as jnp
 from jax import lax
 from jax.sharding import PartitionSpec as P
+
+
+def in_order(blocks, dim):
+    blocks = jnp.moveaxis(blocks, 0, dim)
+    lengths = blocks.shape
+    return blocks.reshape(*lengths[:dim], lengths[dim] * lengths[dim + 1], *lengths[dim + 2 :])
+
+
+def work_both_ways(value, axis, dim, apply, out_dim):
+    size, position, width = (lax.axis_size(axis), lax.axis_index(axis), value.shape[dim])
+    ahead = [(i, (i + 1) % size) for i in range(size)]
+    left = [(i, (i - 1) % size) for i in range(size)]
+    middle = size // 2
+    blocks = {}
+    from_left = from_right = value
+    for step in range(middle + 1):
+        next_left = lax.ppermute(from_left, axis, ahead) if step < middle else None
+        next_right = lax.ppermute(from_right, axis, left) if step < size - middle - 1 else None
+        blocks[-step] = apply(from_left, (position - step) % size * width)
+        if 0 < step < size - middle:
+            blocks[step] = apply(from_right, (position + step) % size * width)
+        from_left, from_right = (next_left, next_right)
+    blocks = jnp.stack([blocks[k] for k in sorted(blocks)])
+    blocks = blocks[(jnp.arange(size) - position + middle) % size]
+    return in_order(blocks, out_dim)
 
 
 def shards(activations, out_grads, query_grads, token_ids, loss_mask):
@@ -9,11 +34,14 @@
     partials = []
     for number in range(blocks):
         gathered = lax.all_gather(activations[number], "out", axis=0, tiled=True)
-        projected = jnp.einsum(
-            "to,qoi->tqi",
-            lax.all_gather(out_grads[number], "inp", axis=0, tiled=True),
-            query_grads,
-            preferred_element_type=jnp.float32,
+        projected = work_both_ways(
+            out_grads[number],
+            "inp",
+            0,
+            lambda own_block, offset: jnp.einsum(
+                "to,qoi->tqi", own_block, query_grads, preferred_element_type=jnp.float32
+            ),
+            0,
         )
         partial_value = jnp.sum(projected * gathered.astype(jnp.float32)[:, None, :], axis=2)
         partial_value = lax.psum(partial_value, ("inp", "out"))

time: 290 us -> 294 us (1.014)
  waiting for transfers between devices: 149 us -> 6.61 us
  matrix products: 77.8 us -> 181 us
  local copies, waits for them, and re-layouts: 6.45 us -> 25.3 us
  other arithmetic: 9.25 us -> 25 us
  starting transfers between devices: 0.12 us -> 7.4 us
    dot_general x2 -> x8, matrix products: 77.8 us -> 181 us  [shards(): jnp.einsum('to,qoi->tqi', own_block, query_grads, preferred_element_type=...]
    all_gather x2, waiting for transfers between devices: 84.5 us -> 0.01 us  [shards(): gathered = lax.all_gather(activations[number], 'out', axis=0, tiled=True)]
    all_gather x2 -> x0, waiting for transfers between devices: 63.4 us -> none  [shards(): lax.all_gather(out_grads[number], 'inp', axis=0, tiled=True)]
    gather x0 -> x2, local copies, waits for them, and re-layouts: none -> 15.4 us  [work_both_ways(): blocks = blocks[(jnp.arange(size) - position + middle) % size]]
    another operation x0 -> x2, other arithmetic: none -> 9.8 us  [work_both_ways(): blocks = jnp.stack([blocks[k] for k in sorted(blocks)])]
    convert_element_type x2 -> x0, other arithmetic: 8.22 us -> none  [shards(): gathered.astype(jnp.float32)[:, None, :]]
    mul x0 -> x2, other arithmetic: none -> 8.13 us  [shards(): projected * gathered.astype(jnp.float32)[:, None, :]]
    ppermute x0 -> x6, starting transfers between devices: none -> 7.36 us  [the longest x4 4.35 us: work_both_ways(): next_left = lax.ppermute(from_left, axis, ahead) if step < middle else None]
  transfers between devices with their start and end apart: 4 -> 8, of which waited for: 4 -> 1; matrix products, arithmetic and copies ran while one was open for 18% -> 63% of each run, Pallas kernels for 0% -> 0%
where the time goes in v1:
time: 294 us; the launch traced here: 293 us
  matrix products  181 us (62%)
  blocking collectives  34.2 us (12%)
  local copies, waits for them, and re-layouts  25.3 us (9%)
  other arithmetic  25 us (9%)
  between operations  13.5 us (5%)
  starting transfers between devices  7.4 us (3%)
  waiting for transfers between devices  6.61 us (2%)
    dot_general x8, matrix products, shards(): jnp.einsum('to,qoi->tqi', own_block, query_grads, preferred_element_type=...  181 us
    psum x1, blocking collectives, shards(): partial_value = lax.psum(partial_value, ('inp', 'out'))  34.2 us
    gather x2, local copies, waits for them, and re-layouts, work_both_ways(): blocks = blocks[(jnp.arange(size) - position + middle) % size]  15.4 us
    another operation x2, other arithmetic, work_both_ways(): blocks = jnp.stack([blocks[k] for k in sorted(blocks)])  9.8 us
    mul x2, other arithmetic, shards(): projected * gathered.astype(jnp.float32)[:, None, :]  8.13 us
    ppermute x4, waiting for transfers between devices, work_both_ways(): next_left = lax.ppermute(from_left, axis, ahead) if step < middle else None  6.57 us
    reduce_sum x2, other arithmetic, shards(): jnp.sum(projected * gathered.astype(jnp.float32)[:, None, :], axis=2)  5.99 us
  transfers between devices with their start and end apart: 8, of which 1 were waited for; matrix products, arithmetic and copies ran while one was open for 63% of the time, Pallas kernels for 0%

profile of v1, /device:TPU:0, one launch (start us, length us, event | category | flops | bytes accessed | tf_op | source)
XLA Modules:
  0.0 293.4 jit_solution(6443480257032775068)
XLA Ops:
  6.5 0.0 all-gather.5.cloned.1.call-start
  6.5 2.3 fusion.13
  8.8 0.0 all-gather.5.cloned.1.call-update
  8.9 0.0 all-gather.7.cloned.1.call-start
  8.9 4.2 %slice_bitcast_fusion.1 = (bf16[128,7168]{1,0:T(8,128)(2,1)}, bf16[128,7168]{1,0:T(8,128)(2,1)}) fusion(bf16[2,128,7168]{2,1,0:T(8,128)(2,1)} %param.6), kind=kLoop, calls=%fused_computation.26 | loop fusion | bytes 7340032 | tf_op jit(solution)/shard_map/squeeze | solution.py:38
  13.1 0.5 collective-permute-start
  13.6 1.9 collective-permute-start.2
  15.5 0.7 collective-permute-start.3
  16.2 1.1 collective-permute-start.5
  17.3 0.0 all-gather.7.cloned.1.call-update
  17.3 0.0 copy-start.8
  17.3 0.0 copy-start.9
  17.3 21.3 %convolution_bitcast_fusion.5 = f32[1,128,2,2048]{3,1,2,0:T(8,128)S(1)} fusion(bf16[2,7168,2048]{2,1,0:T(8,128)(2,1)} %param.7, bf16[2,128,7168]{2,1,0:T(8,128)(2,1)} %param.6), kind=kOutput, calls=%fused_computation.11 | convolution fusion | flops 7516192768 | bytes 62652416 | tf_op jit(solution)/shard_map/to,qoi->tqi/dot_general | solution.py:41
  38.6 0.0 copy-done.8
  38.6 0.4 convert_reduce_fusion
  39.0 0.0 copy-done.9
  39.0 0.6 convert_divide_fusion
  39.7 22.8 %convolution_bitcast_fusion.1 = f32[1,128,2,2048]{3,1,2,0:T(8,128)} fusion(bf16[2,7168,2048]{2,1,0:T(8,128)(2,1)} %param.7, bf16[2,128,7168]{2,1,0:T(8,128)(2,1)} %param.6), kind=kOutput, calls=%fused_computation.7 | convolution fusion | flops 7516192768 | bytes 62652416 | tf_op jit(solution)/shard_map/to,qoi->tqi/dot_general | solution.py:41
  62.5 0.0 collective-permute-done
  62.5 0.7 collective-permute-start.1
  63.1 23.4 %convolution_bitcast_fusion.6 = f32[1,128,2,2048]{3,1,2,0:T(8,128)} fusion(bf16[2,7168,2048]{2,1,0:T(8,128)(2,1)} %param.7, bf16[128,7168]{1,0:T(8,128)(2,1)} %collective-permute-done), kind=kOutput, calls=%fused_computation.12 | convolution fusion | flops 7516192768 | bytes 62652416 | tf_op jit(solution)/shard_map/to,qoi->tqi/dot_general | solution.py:41
  86.6 6.6 %collective-permute-done.3 = bf16[128,7168]{1,0:T(8,128)(2,1)} collective-permute-done((bf16[128,7168]{1,0:T(8,128)(2,1)}, bf16[128,7168]{1,0:T(8,128)(2,1)}, u32[]{:S(2)}, u32[]{:S(2)}) %collective-permute-start.3) | collective-permute-done | bytes 1835040 | tf_op jit(solution)/shard_map/ppermute | solution.py:21
  93.1 2.5 collective-permute-start.4
  95.6 22.7 %convolution_bitcast_fusion.2 = f32[1,128,2,2048]{3,1,2,0:T(8,128)} fusion(bf16[2,7168,2048]{2,1,0:T(8,128)(2,1)} %param.7, bf16[128,7168]{1,0:T(8,128)(2,1)} %collective-permute-done.3), kind=kOutput, calls=%fused_computation.8 | convolution fusion | flops 7516192768 | bytes 62652416 | tf_op jit(solution)/shard_map/to,qoi->tqi/dot_general | solution.py:41
  118.3 0.0 collective-permute-done.2
  118.3 22.7 %convolution_bitcast_fusion.4 = f32[1,128,2,2048]{3,1,2,0:T(8,128)} fusion(bf16[2,7168,2048]{2,1,0:T(8,128)(2,1)} %param.7, bf16[128,7168]{1,0:T(8,128)(2,1)} %collective-permute-done.2), kind=kOutput, calls=%fused_computation.10 | convolution fusion | flops 7516192768 | bytes 62652416 | tf_op jit(solution)/shard_map/to,qoi->tqi/dot_general | solution.py:41
  141.1 0.0 collective-permute-done.5
  141.1 22.7 %convolution_bitcast_fusion = f32[1,128,2,2048]{3,1,2,0:T(8,128)} fusion(bf16[2,7168,2048]{2,1,0:T(8,128)(2,1)} %param.7, bf16[128,7168]{1,0:T(8,128)(2,1)} %collective-permute-done.5), kind=kOutput, calls=%fused_computation.6 | convolution fusion | flops 7516192768 | bytes 62652416 | tf_op jit(solution)/shard_map/to,qoi->tqi/dot_general | solution.py:41
  163.8 4.0 %convert.2 = f32[4,128,2048]{2,1,0:T(8,128)} convert(bf16[4,128,2048]{2,1,0:T(8,128)(2,1)} %bitcast.62) | non-fusion elementwise | flops 1048576 | bytes 6291456 | tf_op jit(solution)/shard_map/mul | solution.py:46
  167.8 4.1 %convert.3 = f32[4,128,2048]{2,1,0:T(8,128)} convert(bf16[4,128,2048]{2,1,0:T(8,128)(2,1)} %bitcast.63) | non-fusion elementwise | flops 1048576 | bytes 6291456 | tf_op jit(solution)/shard_map/mul | solution.py:46
  171.9 0.0 collective-permute-done.1
  171.9 22.9 %convolution_bitcast_fusion.7 = f32[1,128,2,2048]{3,1,2,0:T(8,128)} fusion(bf16[2,7168,2048]{2,1,0:T(8,128)(2,1)} %param.7, bf16[128,7168]{1,0:T(8,128)(2,1)} %collective-permute-done.1), kind=kOutput, calls=%fused_computation.13 | convolution fusion | flops 7516192768 | bytes 62652416 | tf_op jit(solution)/shard_map/to,qoi->tqi/dot_general | solution.py:41
  194.8 0.0 copy-done.4
  194.8 0.0 copy-done.6
  194.8 5.0 %pad_maximum_fusion = f32[4,128,2,2048]{3,1,2,0:T(8,128)} fusion(f32[1,128,2,2048]{3,1,2,0:T(8,128)S(1)} %copy-done.6, f32[1,128,2,2048]{3,1,2,0:T(8,128)S(1)} %convolution_bitcast_fusion.5, f32[1,128,2,2048]{3,1,2,0:T(8,128)S(1)} %copy-done.4, f32[1,128,2,2048]{3,1,2,0:T(8,128)} %convolution_bitcast_fusion.7), kind=kLoop, calls=%fused_computation.2 | loop fusion | flops 6291456 | bytes 16777216 | tf_op jit(solution)/shard_map/stack | solution.py:27
  199.8 7.7 %gather_fusion = f32[4,128,2,2048]{3,1,2,0:T(8,128)} fusion(f32[4,128,2,2048]{3,1,2,0:T(8,128)} %pad_maximum_fusion, s32[1024]{0:T(1024)S(1)} %pad_clamp_fusion), kind=kCustom, calls=%fused_computation | custom fusion | bytes 16777232 | tf_op jit(solution)/shard_map/gather | solution.py:28
  207.5 0.0 collective-permute-done.4
  207.5 22.9 %convolution_bitcast_fusion.3 = f32[1,128,2,2048]{3,1,2,0:T(8,128)} fusion(bf16[2,7168,2048]{2,1,0:T(8,128)(2,1)} %param.7, bf16[128,7168]{1,0:T(8,128)(2,1)} %collective-permute-done.4), kind=kOutput, calls=%fused_computation.9 | convolution fusion | flops 7516192768 | bytes 62652416 | tf_op jit(solution)/shard_map/to,qoi->tqi/dot_general | solution.py:41
  230.4 0.0 copy-done.2
  230.4 0.0 copy-done.3
  230.4 4.8 %pad_maximum_fusion.1 = f32[4,128,2,2048]{3,1,2,0:T(8,128)} fusion(f32[1,128,2,2048]{3,1,2,0:T(8,128)S(1)} %copy-done.5, f32[1,128,2,2048]{3,1,2,0:T(8,128)S(1)} %copy-done.2, f32[1,128,2,2048]{3,1,2,0:T(8,128)S(1)} %copy-done.3, f32[1,128,2,2048]{3,1,2,0:T(8,128)} %convolution_bitcast_fusion.3), kind=kLoop, calls=%fused_computation.3 | loop fusion | flops 6291456 | bytes 16777216 | tf_op jit(solution)/shard_map/stack | solution.py:27
  235.2 7.7 %gather_fusion.1 = f32[4,128,2,2048]{3,1,2,0:T(8,128)} fusion(f32[4,128,2,2048]{3,1,2,0:T(8,128)} %pad_maximum_fusion.1, s32[1024]{0:T(1024)S(1)} %pad_clamp_fusion), kind=kCustom, calls=%fused_computation.1 | custom fusion | bytes 16777232 | tf_op jit(solution)/shard_map/gather | solution.py:28
  242.9 5.4 %multiply_reduce_fusion.1 = f32[4,128,2]{1,2,0:T(2,128)S(1)} fusion(f32[4,128,2,2048]{3,1,2,0:T(8,128)} %gather_fusion, f32[4,128,2048]{2,1,0:T(8,128)} %convert.2), kind=kLoop, calls=%fused_computation.5 | loop fusion | flops 4193280 | bytes 12587008 | tf_op jit(solution)/shard_map/reduce_sum | solution.py:46
  248.3 1.6 copy-done
  249.9 1.2 copy-done.1
  251.1 0.6 multiply_reduce_fusion
  251.7 34.2 %all-reduce = (f32[1,512,2]{1,2,0:T(2,128)S(1)}, f32[1,512,2]{1,2,0:T(2,128)S(1)}) all-reduce(f32[1,512,2]{1,2,0:T(2,128)S(1)} %bitcast.65, f32[1,512,2]{1,2,0:T(2,128)S(1)} %bitcast.64), channel_id=1, replica_groups=mesh['grp'=2,'inp'=4,'out'=4] {'inp','out'}, use_global_device_ids=true, to_apply=%region_3.4 | all-reduce | flops 2048 | bytes 16384 | tf_op jit(solution)/shard_map/psum | solution.py:47
  285.9 0.6 copy.7
  (15 shorter events, 0.0 us)
Async XLA Ops:
  6.5 157.3 %all-gather.5.cloned.1.call-start = ((), (), s32[]{:S(2)}) async-start(), calls=%async_computation | async-start | bytes 2621440 | tf_op jit(solution)/shard_map/all_gather | solution.py:36
  8.9 159.0 %all-gather.7.cloned.1.call-start = ((), (), s32[]{:S(2)}) async-start(), calls=%async_computation.1 | async-start | bytes 2621440 | tf_op jit(solution)/shard_map/all_gather | solution.py:36
  13.1 49.4 %collective-permute-start = (bf16[128,7168]{1,0:T(8,128)(2,1)}, bf16[128,7168]{1,0:T(8,128)(2,1)}, u32[]{:S(2)}, u32[]{:S(2)}) collective-permute-start(bf16[128,7168]{1,0:T(8,128)(2,1)} %get-tuple-element.7), channel_id=1, source_target_pairs={{0,4},{4,8},{8,12},{12,0},{1,5},{5,9},{9,13},{13,1},{2,6},{6,10},{... | collective-permute-start | bytes 5505032 | tf_op jit(solution)/shard_map/ppermute | solution.py:21
  13.6 104.8 %collective-permute-start.2 = (bf16[128,7168]{1,0:T(8,128)(2,1)}, bf16[128,7168]{1,0:T(8,128)(2,1)}, u32[]{:S(2)}, u32[]{:S(2)}) collective-permute-start(bf16[128,7168]{1,0:T(8,128)(2,1)} %get-tuple-element.7), channel_id=1, source_target_pairs={{0,12},{4,0},{8,4},{12,8},{1,13},{5,1},{9,5},{13,9},{2,14},{6,2},{... | collective-permute-start | bytes 5505032 | tf_op jit(solution)/shard_map/ppermute | solution.py:22
  15.5 77.6 %collective-permute-start.3 = (bf16[128,7168]{1,0:T(8,128)(2,1)}, bf16[128,7168]{1,0:T(8,128)(2,1)}, u32[]{:S(2)}, u32[]{:S(2)}) collective-permute-start(bf16[128,7168]{1,0:T(8,128)(2,1)} %get-tuple-element.8), channel_id=1, source_target_pairs={{0,4},{4,8},{8,12},{12,0},{1,5},{5,9},{9,13},{13,1},{2,6},{6,10},{... | collective-permute-start | bytes 5505032 | tf_op jit(solution)/shard_map/ppermute | solution.py:21
  16.2 124.9 %collective-permute-start.5 = (bf16[128,7168]{1,0:T(8,128)(2,1)}, bf16[128,7168]{1,0:T(8,128)(2,1)}, u32[]{:S(2)}, u32[]{:S(2)}) collective-permute-start(bf16[128,7168]{1,0:T(8,128)(2,1)} %get-tuple-element.8), channel_id=1, source_target_pairs={{0,12},{4,0},{8,4},{12,8},{1,13},{5,1},{9,5},{13,9},{2,14},{6,2},{... | collective-permute-start | bytes 5505032 | tf_op jit(solution)/shard_map/ppermute | solution.py:22
  17.3 21.3 %copy-start.8 = (s32[2,512]{1,0:T(2,128)S(1)}, s32[2,512]{1,0:T(2,128)}, u32[]{:S(2)}) copy-start(s32[2,512]{1,0:T(2,128)} %param.8) | copy-start | bytes 12292
  17.3 21.7 %copy-start.9 = (s32[2,512]{1,0:T(2,128)S(1)}, s32[2,512]{1,0:T(2,128)}, u32[]{:S(2)}) copy-start(s32[2,512]{1,0:T(2,128)} %param.9) | copy-start | bytes 12292
  62.5 109.5 %collective-permute-start.1 = (bf16[128,7168]{1,0:T(8,128)(2,1)}, bf16[128,7168]{1,0:T(8,128)(2,1)}, u32[]{:S(2)}, u32[]{:S(2)}) collective-permute-start(bf16[128,7168]{1,0:T(8,128)(2,1)} %collective-permute-done), channel_id=1, source_target_pairs={{0,4},{4,8},{8,12},{12,0},{1,5},{5,9},{9,13},{13,1},{2,6},{6,10},{... | collective-permute-start | bytes 5505032 | tf_op jit(solution)/shard_map/ppermute | solution.py:21
  93.1 114.4 %collective-permute-start.4 = (bf16[128,7168]{1,0:T(8,128)(2,1)}, bf16[128,7168]{1,0:T(8,128)(2,1)}, u32[]{:S(2)}, u32[]{:S(2)}) collective-permute-start(bf16[128,7168]{1,0:T(8,128)(2,1)} %collective-permute-done.3), channel_id=1, source_target_pairs={{0,4},{4,8},{8,12},{12,0},{1,5},{5,9},{9,13},{13,1},{2,6},{6,10},{... | collective-permute-start | bytes 5505032 | tf_op jit(solution)/shard_map/ppermute | solution.py:21
  171.9 22.9 %copy-start.4 = (f32[1,128,2,2048]{3,1,2,0:T(8,128)S(1)}, f32[1,128,2,2048]{3,1,2,0:T(8,128)}, u32[]{:S(2)}) copy-start(f32[1,128,2,2048]{3,1,2,0:T(8,128)} %convolution_bitcast_fusion.6) | copy-start | bytes 6291460
  171.9 22.9 %copy-start.6 = (f32[1,128,2,2048]{3,1,2,0:T(8,128)S(1)}, f32[1,128,2,2048]{3,1,2,0:T(8,128)}, u32[]{:S(2)}) copy-start(f32[1,128,2,2048]{3,1,2,0:T(8,128)} %convolution_bitcast_fusion.4) | copy-start | bytes 6291460
  207.5 22.9 %copy-start.2 = (f32[1,128,2,2048]{3,1,2,0:T(8,128)S(1)}, f32[1,128,2,2048]{3,1,2,0:T(8,128)}, u32[]{:S(2)}) copy-start(f32[1,128,2,2048]{3,1,2,0:T(8,128)} %convolution_bitcast_fusion.1) | copy-start | bytes 6291460
  207.5 22.9 %copy-start.3 = (f32[1,128,2,2048]{3,1,2,0:T(8,128)S(1)}, f32[1,128,2,2048]{3,1,2,0:T(8,128)}, u32[]{:S(2)}) copy-start(f32[1,128,2,2048]{3,1,2,0:T(8,128)} %convolution_bitcast_fusion.2) | copy-start | bytes 6291460
  207.5 22.9 %copy-start.5 = (f32[1,128,2,2048]{3,1,2,0:T(8,128)S(1)}, f32[1,128,2,2048]{3,1,2,0:T(8,128)}, u32[]{:S(2)}) copy-start(f32[1,128,2,2048]{3,1,2,0:T(8,128)} %convolution_bitcast_fusion) | copy-start | bytes 6291460
  242.9 7.0 %copy-start = (f32[4,128,2,2048]{3,1,2,0:T(8,128)S(1)}, f32[4,128,2,2048]{3,1,2,0:T(8,128)}, u32[]{:S(2)}) copy-start(f32[4,128,2,2048]{3,1,2,0:T(8,128)} %gather_fusion.1) | copy-start | bytes 25165828
  242.9 8.2 %copy-start.1 = (f32[4,128,2048]{2,1,0:T(8,128)S(1)}, f32[4,128,2048]{2,1,0:T(8,128)}, u32[]{:S(2)}) copy-start(f32[4,128,2048]{2,1,0:T(8,128)} %convert.3) | copy-start | bytes 12582916
  251.1 34.8 %copy-start.7 = (f32[2,512]{1,0:T(2,128)S(1)}, f32[2,512]{1,0:T(2,128)}, u32[]{:S(2)}) copy-start(f32[2,512]{1,0:T(2,128)} %convert_divide_fusion) | copy-start | bytes 12292
Sparse Core Ops, SparseCore 0:
  9.0 48.3 all-gather.4
  59.0 44.4 all-gather.6
